TPU v7x, 256 devices: a whole 4x4x8 slice. The times are simulated.
256 devices in a mesh: blk: 64 (over z, y, core), layer: 4 (over x).
Axes of the slice: x: 4, y: 4, z: 8, core: 2. Of those that a mesh axis runs over, the one named last changes fastest.
Arguments:
- leaf_area: float32 [12, 16, 8192], P(None, 'layer', 'blk'), may hold values from 0 to 6
- soil_water: float32 [10, 8192], P(None, 'blk'), may hold values from 0.05 to 0.5
- root_share: float32 [16, 10], P('layer'), may hold values from 0 to 0.3
- patch_weight: float32 [16, 262144], P('layer', 'blk'), may hold values from 0 to 1
- patch_owner: int32 [262144, 1], P('blk'), may hold values from 0 to 63; in each aligned block of 4096 rows (0 to 4095, 4096 to 8191, ...) at most 128 rows name the same one
- patch_local: int32 [262144], P('blk'), may hold values from 0 to 127
- month: int32 [1], replicated, may hold values from 0 to 11
- mix: float32 [1], replicated, may hold values from 0.1 to 0.9
Outputs:
- canopy_share: float32 [16, 8192], P('layer', 'blk')
Inputs may be any that keep to these rules, and one draw needn't show every extreme that they name: `patch_owner`: among the rows of one device, no owner is named more than 128 times, a bound that some block reaches.
All inputs are finite; a program needn't handle non-finite values.
Results may differ from a plain program's by a relative error of at most 0.000065.
Values sent between devices are 32-bit elements; how exact they have to be, the bound alone decides.
No kernel may reach another device: no remote copies, remote signals or barrier semaphores. Data moves between devices by JAX's collectives and lax.ppermute only.
A program may use at most 64 MiB of HBM per device.

v0:
```python
import jax
import jax.numpy as jnp
from jax import lax
from jax.sharding import PartitionSpec as P


def gathered_total(x, axis):
    tiles = lax.all_gather(x, axis)
    return tiles.sum(axis=0)


def interpolate(leaf_area, month, mix):
    earlier_index = month[0]
    second = (earlier_index + 1) % leaf_area.shape[0]
    earlier = lax.dynamic_index_in_dim(leaf_area, earlier_index, 0, keepdims=False)
    later = lax.dynamic_index_in_dim(leaf_area, second, 0, keepdims=False)
    return mix[0] * earlier + (1.0 - mix[0]) * later


def exact_dot(left, right):
    return jnp.dot(left, right, precision=lax.Precision.HIGHEST)


def on_device(
    leaf_area, soil_water, root_share, patch_weight, patch_owner, patch_local, month, mix
):
    months_count, types_here, cells_here = leaf_area.shape
    patch_count = patch_local.shape[0]
    owners = patch_owner[:, 0]
    cell_iota = jnp.arange(cells_here, dtype=jnp.int32)
    devices = lax.axis_size("blk")
    capacity = max(2, 2 * patch_count // devices)
    owner_table = (owners[:, None] == jnp.arange(devices, dtype=jnp.int32)[None, :]).astype(
        jnp.float32
    )
    patch_iota = jnp.arange(patch_count, dtype=jnp.int32)
    earlier = (patch_iota[:, None] > patch_iota[None, :]).astype(jnp.float32)
    before = exact_dot(earlier, owner_table)
    ranks = jnp.sum(before * owner_table, axis=1).astype(jnp.int32)
    slots = owners * capacity + ranks
    slot_iota = jnp.arange(devices * capacity, dtype=jnp.int32)
    slot_table = (slots[:, None] == slot_iota[None, :]).astype(jnp.float32)
    packed = jnp.concatenate([patch_weight, patch_local.astype(jnp.float32)[None, :]], axis=0)
    buffer = exact_dot(packed, slot_table)
    received = lax.all_to_all(buffer, "blk", split_axis=1, concat_axis=1, tiled=True)
    weights = received[:types_here]
    cell_ids = received[types_here].astype(jnp.int32)
    cell_table = (cell_iota[:, None] == cell_ids[None, :]).astype(jnp.float32)
    current = interpolate(leaf_area, month, mix)
    cell_stress = exact_dot(root_share, soil_water)
    factor = (1.0 - jnp.exp(-0.5 * current)) * cell_stress
    canopy = weights * exact_dot(factor, cell_table)
    grid_sum = exact_dot(canopy, cell_table.T)
    total = gathered_total(jnp.sum(grid_sum, axis=0), "layer")
    return grid_sum / (1.0 + total)


def solution(mesh):
    in_specs = (
        P(None, "layer", "blk"),
        P(None, "blk"),
        P("layer", None),
        P("layer", "blk"),
        P("blk", None),
        P("blk"),
        P(),
        P(),
    )
    out_specs = P("layer", "blk")
    return jax.shard_map(
        on_device, mesh=mesh, in_specs=in_specs, out_specs=out_specs, check_vma=False
    )
```

profile of v0, /device:TPU:8, one launch (start us, length us, event | category | flops | bytes accessed | tf_op | source)
XLA Modules:
  0.0 101.2 jit_solution(8388611021400690604)
XLA Ops:
  0.0 0.0 copy-start
  0.0 0.7 convert_element_type.30
  0.7 0.0 copy-start.2
  0.7 0.0 copy-start.1
  0.7 19.1 %fusion.7 = f32[4096]{0:T(1024)S(1)} fusion(s32[4096]{0:T(1024)} %bitcast.33), kind=kOutput, calls=%fused_computation.11 | convolution fusion | flops 2165305344 | bytes 32768 | tf_op jit(solution)/shard_map/dot_general | solution.py:21
  19.9 0.0 copy-done.2
  19.9 0.0 copy-done.1
  19.9 43.1 %fusion.8 = f32[5,64,128]{2,0,1:T(8,128)} fusion(s32[4096]{0:T(1024)S(1)} %bitcast.34, f32[5,4096]{1,0:T(8,128)S(1)} %fusion.22), kind=kOutput, calls=%fused_computation.12 | convolution fusion | flops 2046820352 | bytes 262144 | tf_op jit(solution)/shard_map/dot_general | solution.py:21
  63.0 0.0 copy-start.3
  63.1 12.2 %all-to-all-start = ((f32[5,64,128]{2,0,1:T(8,128)}), f32[5,64,128]{2,0,1:T(8,128)S(1)}, u32[]{:S(2)}, u32[]{:S(2)}) async-start(f32[5,64,128]{2,0,1:T(8,128)} %fusion.8), calls=%async_computation | async-start | bytes 524288 | tf_op jit(solution)/shard_map/all_to_all | solution.py:45
  76.6 0.0 copy-done
  76.6 0.0 copy-done.3
  76.6 0.8 convolution_multiply_fusion.1
  77.5 10.0 %all-to-all-done = f32[5,64,128]{2,0,1:T(8,128)S(1)} async-done(((f32[5,64,128]{2,0,1:T(8,128)}), f32[5,64,128]{2,0,1:T(8,128)S(1)}, u32[]{:S(2)}, u32[]{:S(2)}) %all-to-all-start) | async-done | bytes 163872 | tf_op jit(solution)/shard_map/all_to_all | solution.py:45
  87.6 1.4 %convolution_multiply_fusion = f32[4,8192]{1,0:T(4,128)S(1)} fusion(f32[4,128]{1,0:T(4,128)S(1)} %convolution_multiply_fusion.1, s32[8192]{0:T(1024)S(1)} %bitcast.31, f32[5,64,128]{2,0,1:T(8,128)S(1)} %all-to-all-done), kind=kOutput, calls=%fused_computation.5 | convolution fusion | flops 51412992 | bytes 296960 | tf_op jit(solution)/shard_map/dot_general | solution.py:21
  89.0 2.0 %fusion.14 = (f32[128]{0:T(128)S(1)}, f32[4,128]{1,0:T(4,128)S(1)}) fusion(f32[4,8192]{1,0:T(4,128)S(1)} %convolution_multiply_fusion, s32[8192]{0:T(1024)S(1)} %bitcast.32), kind=kOutput, calls=%fused_computation.25 | convolution fusion | flops 51380608 | bytes 166400 | tf_op jit(solution)/shard_map/dot_general | solution.py:21
  91.0 9.7 %all-gather.1 = f32[4,1,128]{2,1,0:T(1,128)S(1)} all-gather(f32[1,1,128]{2,1,0:T(1,128)S(1)} %bitcast.35), channel_id=2, replica_groups=mesh['blk'=64,'layer'=4] {'layer'}, dimensions={0}, use_global_device_ids=true | all-gather | bytes 2560 | tf_op jit(solution)/shard_map/all_gather | solution.py:8
  100.6 0.6 broadcast_divide_fusion
  (6 shorter events, 0.1 us)
Async XLA Ops:
  0.0 76.6 %copy-start = (f32[10,128]{1,0:T(8,128)S(1)}, f32[10,128]{1,0:T(8,128)}, u32[]{:S(2)}) copy-start(f32[10,128]{1,0:T(8,128)} %param.9) | copy-start | bytes 15364
  0.7 19.1 %copy-start.2 = (s32[4096,1]{0,1:T(1,128)S(1)}, s32[4096,1]{0,1:T(1,128)}, u32[]{:S(2)}) copy-start(s32[4096,1]{0,1:T(1,128)} %param.12) | copy-start | bytes 49156
  0.7 19.2 %copy-start.1 = (f32[4,4096]{1,0:T(4,128)S(1)}, f32[4,4096]{1,0:T(4,128)}, u32[]{:S(2)}) copy-start(f32[4,4096]{1,0:T(4,128)} %param.11) | copy-start | bytes 196612
  63.0 13.6 %copy-start.3 = (f32[4,10]{1,0:T(4,128)S(1)}, f32[4,10]{1,0:T(4,128)}, u32[]{:S(2)}) copy-start(f32[4,10]{1,0:T(4,128)} %param.10) | copy-start | bytes 484
  63.1 24.5 %all-to-all-start = ((f32[5,64,128]{2,0,1:T(8,128)}), f32[5,64,128]{2,0,1:T(8,128)S(1)}, u32[]{:S(2)}, u32[]{:S(2)}) async-start(f32[5,64,128]{2,0,1:T(8,128)} %fusion.8), calls=%async_computation | async-start | bytes 524288 | tf_op jit(solution)/shard_map/all_to_all | solution.py:45
where the time goes:
time: 102 us; the launch traced here: 101 us
  matrix products  66.4 us (65%)
  starting transfers between devices  12.2 us (12%)
  waiting for transfers between devices  10 us (10%)
  blocking collectives  9.66 us (9%)
  other arithmetic  1.45 us (1%)
  between operations  1.39 us (1%)
    dot_general x5, matrix products, exact_dot(): return jnp.dot(left, right, precision=lax.Precision.HIGHEST)  66.4 us
    all_to_all x1, starting transfers between devices, on_device(): lax.all_to_all(buffer, 'blk', split_axis=1, concat_axis=1, tiled=True)  12.2 us
    all_to_all x1, waiting for transfers between devices, on_device(): lax.all_to_all(buffer, 'blk', split_axis=1, concat_axis=1, tiled=True)  10 us
    all_gather x1, blocking collectives, gathered_total(): tiles = lax.all_gather(x, axis)  9.66 us
  transfers between devices with their start and end apart: 1, of which 1 were waited for; matrix products, arithmetic and copies ran while one was open for 1% of the time, Pallas kernels for 0%

commit v1 on v0

v1 whole, which is shorter than its diff:
```python
import jax
import jax.numpy as jnp
from jax import lax
from jax.experimental import pallas as pl
from jax.experimental.pallas import tpu as pltpu
from jax.sharding import Mesh
from jax.sharding import PartitionSpec as P

F32 = jnp.float32
BF16 = jnp.bfloat16
CHUNK = 256
CELLS = 128


def vmem():
    return pl.BlockSpec(memory_space=pltpu.VMEM)


def limit(mib):
    return pltpu.CompilerParams(vmem_limit_bytes=mib << 20)


def smem():
    return pl.BlockSpec(memory_space=pltpu.SMEM)


def weight_sums_kernel(core_ref, weight_ref, owner_ref, local_ref, send_ref, keep_ref):
    types, patches = weight_ref.shape
    rows = send_ref.shape[0]
    chips = rows // types
    row_chip = lax.broadcasted_iota(jnp.int32, (rows, CHUNK), 0) // types
    row_chip = row_chip.astype(F32).astype(BF16)
    column = lax.broadcasted_iota(jnp.int32, (2 * CELLS, CHUNK), 0).astype(F32).astype(BF16)
    zero = jnp.zeros((), BF16)
    one = jnp.ones((), BF16)
    total = jnp.zeros((2 * rows, 2 * CELLS), F32)
    for step in range(patches // CHUNK):
        part = pl.ds(step * CHUNK, CHUNK)
        owner = owner_ref[:, part]
        chip = (owner >> 1).astype(F32).astype(BF16)
        place = ((owner & 1) * CELLS + local_ref[:, part]).astype(F32).astype(BF16)
        weight = weight_ref[:, part]
        high = weight.astype(BF16)
        low = (weight - high.astype(F32)).astype(BF16)
        named = jnp.broadcast_to(chip, (rows, CHUNK)) == row_chip
        left = jnp.concatenate(
            [
                jnp.where(named, jnp.concatenate([high] * chips, axis=0), zero),
                jnp.where(named, jnp.concatenate([low] * chips, axis=0), zero),
            ],
            axis=0,
        )
        right = jnp.where(jnp.broadcast_to(place, (2 * CELLS, CHUNK)) == column, one, zero)
        total += lax.dot_general(
            left, right, (((1,), (1,)), ((), ())), preferred_element_type=F32
        )
    both = total[:rows] + total[rows:]
    first, second = both[:, :CELLS], both[:, CELLS:]
    low_core = core_ref[0] == 0
    send_ref[...] = jnp.where(low_core, second, first)
    keep_ref[...] = jnp.where(low_core, first, second)


def weight_sums(core, weight, owner, local, chips):
    types, patches = weight.shape
    shape = jax.ShapeDtypeStruct((chips * types, CELLS), F32)
    return pl.pallas_call(
        weight_sums_kernel,
        out_shape=[shape, shape],
        in_specs=[smem(), vmem(), vmem(), vmem()],
        out_specs=[vmem(), vmem()],
        compiler_params=limit(8),
        name="weight_sums",
    )(core, weight, owner, local)


def factor_kernel(month_ref, mix_ref, leaf_ref, soil_ref, root_ref, factor_ref):
    earlier = month_ref[0]
    later = (earlier + 1) % leaf_ref.shape[0]
    mix = mix_ref[0]
    current = mix * leaf_ref[earlier] + (1.0 - mix) * leaf_ref[later]
    stress = jnp.zeros_like(current)
    for layer in range(soil_ref.shape[0]):
        stress += root_ref[:, layer : layer + 1] * soil_ref[layer : layer + 1, :]
    factor_ref[...] = (1.0 - jnp.exp(-0.5 * current)) * stress


def cell_factor(month, mix, leaf_area, soil_water, root_share):
    return pl.pallas_call(
        factor_kernel,
        out_shape=jax.ShapeDtypeStruct(leaf_area.shape[1:], F32),
        in_specs=[smem(), smem(), vmem(), vmem(), vmem()],
        out_specs=vmem(),
        compiler_params=limit(1),
        name="cell_factor",
    )(month, mix, leaf_area, soil_water, root_share)


def grid_sum_kernel(received_ref, factor_ref, grid_sum_ref, total_ref):
    grid_sum = jnp.sum(received_ref[...], axis=0) * factor_ref[...]
    grid_sum_ref[...] = grid_sum
    total_ref[...] = jnp.sum(grid_sum, axis=0, keepdims=True)


def share_kernel(grid_sum_ref, total_ref, *rest):
    *others, share_ref = rest
    total = total_ref[...]
    for other in others:
        total += other[...]
    share_ref[...] = grid_sum_ref[...] / (1.0 + total)


def on_device(
    leaf_area, soil_water, root_share, patch_weight, patch_owner, patch_local, month, mix
):
    types = leaf_area.shape[1]
    chips = lax.axis_size("z") * lax.axis_size("y")
    layers = lax.axis_size("x")
    core = lax.axis_index("core").astype(jnp.int32).reshape(1)
    send, keep = weight_sums(
        core, patch_weight, patch_owner.reshape(1, -1), patch_local.reshape(1, -1), chips
    )
    sums = keep + lax.ppermute(send, "core", [(0, 1), (1, 0)])
    received = lax.all_to_all(
        sums.reshape(chips, types, CELLS), ("z", "y"), split_axis=0, concat_axis=0, tiled=True
    )
    factor = cell_factor(month, mix, leaf_area, soil_water, root_share)
    grid_sum, total = pl.pallas_call(
        grid_sum_kernel,
        out_shape=[
            jax.ShapeDtypeStruct((types, CELLS), F32),
            jax.ShapeDtypeStruct((1, CELLS), F32),
        ],
        in_specs=[vmem(), vmem()],
        out_specs=[vmem(), vmem()],
        compiler_params=limit(1),
        name="grid_sum",
    )(received, factor)
    others = [
        lax.ppermute(total, "x", [(i, (i + hop) % layers) for i in range(layers)])
        for hop in range(1, layers)
    ]
    return pl.pallas_call(
        share_kernel,
        out_shape=jax.ShapeDtypeStruct((types, CELLS), F32),
        in_specs=[vmem()] * (1 + layers),
        out_specs=vmem(),
        compiler_params=limit(1),
        name="canopy_share",
    )(grid_sum, total, *others)


def solution(mesh):
    blk = ("z", "y", "core")
    inner = Mesh(mesh.devices.reshape(8, 4, 2, 4), (*blk, "x"))
    in_specs = (
        P(None, "x", blk),
        P(None, blk),
        P("x", None),
        P("x", blk),
        P(blk, None),
        P(blk),
        P(),
        P(),
    )
    return jax.shard_map(
        on_device, mesh=inner, in_specs=in_specs, out_specs=P("x", blk), check_vma=False
    )
```

time: 102 us -> 35.3 us (0.35)
  the two profiles are of different devices: /device:TPU:8 before, /device:TPU:6 now
where the time goes in v1:
time: 35.3 us; the launch traced here: 35 us
  starting transfers between devices  14.7 us (42%)
  waiting for transfers between devices  14.5 us (41%)
  local copies, waits for them, and re-layouts  2.29 us (6%)
  Pallas kernels  1.47 us (4%)
  between operations  1.37 us (4%)
  other arithmetic  0.63 us (2%)
    all_to_all x1, starting transfers between devices, on_device(): lax.all_to_all(sums.reshape(chips, types, CELLS), ('z', 'y'), split_axis=...  11.6 us
    all_to_all x1, waiting for transfers between devices, on_device(): lax.all_to_all(sums.reshape(chips, types, CELLS), ('z', 'y'), split_axis=...  8.54 us
    ppermute x3, waiting for transfers between devices, on_device(): lax.ppermute(total, 'x', [(i, (i + hop) % layers) for i in range(layers)])  4.75 us
    ppermute x3, starting transfers between devices, on_device(): lax.ppermute(total, 'x', [(i, (i + hop) % layers) for i in range(layers)])  2.98 us
    unnamed x12, local copies, waits for them, and re-layouts  2.29 us
    ppermute x1, waiting for transfers between devices, on_device(): sums = keep + lax.ppermute(send, 'core', [(0, 1), (1, 0)])  1.24 us
    pallas_call x1, Pallas kernels, weight_sums(): pl.pallas_call(weight_sums_kernel, out_shape=[shape, shape], in_specs=[sm...  0.75 us
  transfers between devices with their start and end apart: 5, of which 5 were waited for; matrix products, arithmetic and copies ran while one was open for 0% of the time, Pallas kernels for 0%

profile of v1, /device:TPU:6, one launch (start us, length us, event | category | flops | bytes accessed | tf_op | source)
XLA Modules:
  0.0 35.0 jit_solution(10277032158525800328)
XLA Ops:
  0.0 0.0 copy-start
  0.0 0.8 %copy-done = f32[4,4096]{1,0:T(4,128)S(1)} copy-done((f32[4,4096]{1,0:T(4,128)S(1)}, f32[4,4096]{1,0:T(4,128)}, u32[]{:S(2)}) %copy-start) | copy-done | bytes 65560
  0.8 0.0 copy-start.2
  0.8 0.7 %copy-done.2 = s32[4096,1]{0,1:T(1,128)S(1)} copy-done((s32[4096,1]{0,1:T(1,128)S(1)}, s32[4096,1]{0,1:T(1,128)}, u32[]{:S(2)}) %copy-start.2) | copy-done | bytes 16408
  1.6 0.7 %copy-done.3 = s32[4096]{0:T(1024)S(1)} copy-done((s32[4096]{0:T(1024)S(1)}, s32[4096]{0:T(1024)}, u32[]{:S(2)}) %copy-start.3) | copy-done | bytes 16408
  2.3 0.8 %weight_sums.1 = (f32[128,128]{1,0:T(8,128)S(1)}, f32[128,128]{1,0:T(8,128)S(1)}) custom-call(s32[1]{0:T(128)} %bitcast.core_ref, f32[4,4096]{1,0:T(4,128)S(1)} %copy-done, s32[1,4096]{1,0:T(1,128)S(1)} %bitcast.4, s32[1,4096]{1,0:T(1,128)S(1)} %bitcast.5), custom_call_target="tpu_custom_call" | custom-call | tf_op jit(solution)/shard_map/weight_sums/pallas_call | solution.py:67
  3.0 0.1 collective-permute-start
  3.1 1.2 %collective-permute-done = f32[128,128]{1,0:T(8,128)S(1)} collective-permute-done((f32[128,128]{1,0:T(8,128)S(1)}, f32[128,128]{1,0:T(8,128)S(1)}, u32[]{:S(2)}, u32[]{:S(2)}) %collective-permute-start) | collective-permute-done | bytes 65568 | tf_op jit(solution)/shard_map/ppermute | solution.py:123
  4.4 0.6 %add.3 = f32[128,128]{1,0:T(8,128)} add(f32[128,128]{1,0:T(8,128)S(1)} %get-tuple-element.9, f32[128,128]{1,0:T(8,128)S(1)} %collective-permute-done) | non-fusion elementwise | flops 16384 | bytes 196608 | tf_op jit(solution)/shard_map/add | solution.py:123
  5.0 0.0 copy-start.1
  5.0 11.6 %all-to-all-start = ((f32[32,4,128]{2,1,0:T(4,128)}), f32[32,4,128]{2,1,0:T(4,128)S(1)}, u32[]{:S(2)}, u32[]{:S(2)}) async-start(f32[32,4,128]{2,1,0:T(4,128)} %bitcast.3), calls=%async_computation | async-start | bytes 131072 | tf_op jit(solution)/shard_map/all_to_all | solution.py:124
  16.6 0.0 copy-start.5
  18.0 0.0 copy-done.1
  18.0 0.0 copy-done.4
  18.0 0.0 copy-done.5
  18.0 0.1 cell_factor.1.factor_ref
  18.1 8.5 %all-to-all-done.received_ref = f32[32,4,128]{2,1,0:T(4,128)S(1)} async-done(((f32[32,4,128]{2,1,0:T(4,128)}), f32[32,4,128]{2,1,0:T(4,128)S(1)}, u32[]{:S(2)}, u32[]{:S(2)}) %all-to-all-start) | async-done | bytes 65568 | tf_op jit(solution)/shard_map/all_to_all | solution.py:124
  26.6 0.5 %collective-permute-start.1 = (f32[1,128]{1,0:T(1,128)S(1)}, f32[1,128]{1,0:T(1,128)S(1)}, u32[]{:S(2)}, u32[]{:S(2)}) collective-permute-start(f32[1,128]{1,0:T(1,128)S(1)} %get-tuple-element.12.total_ref), channel_id=1, source_target_pairs={{0,1},{1,2},{2,3},{3,0},{4,5},{5,6},{6,7},{7,4},{8,9},{9,10},{10,1... | collective-permute-start | bytes 1544 | tf_op jit(solution)/shard_map/ppermute | solution.py:140
  27.2 2.4 %collective-permute-start.2 = (f32[1,128]{1,0:T(1,128)S(1)}, f32[1,128]{1,0:T(1,128)S(1)}, u32[]{:S(2)}, u32[]{:S(2)}) collective-permute-start(f32[1,128]{1,0:T(1,128)S(1)} %get-tuple-element.12.total_ref), channel_id=1, source_target_pairs={{0,2},{1,3},{2,0},{3,1},{4,6},{5,7},{6,4},{7,5},{8,10},{9,11},{10,... | collective-permute-start | bytes 1544 | tf_op jit(solution)/shard_map/ppermute | solution.py:140
  29.6 0.0 collective-permute-start.3
  29.6 0.6 %collective-permute-done.1.rest_0_ = f32[1,128]{1,0:T(1,128)S(1)} collective-permute-done((f32[1,128]{1,0:T(1,128)S(1)}, f32[1,128]{1,0:T(1,128)S(1)}, u32[]{:S(2)}, u32[]{:S(2)}) %collective-permute-start.1) | collective-permute-done | bytes 544 | tf_op jit(solution)/shard_map/ppermute | solution.py:140
  30.3 2.0 %collective-permute-done.2.rest_1_ = f32[1,128]{1,0:T(1,128)S(1)} collective-permute-done((f32[1,128]{1,0:T(1,128)S(1)}, f32[1,128]{1,0:T(1,128)S(1)}, u32[]{:S(2)}, u32[]{:S(2)}) %collective-permute-start.2) | collective-permute-done | bytes 544 | tf_op jit(solution)/shard_map/ppermute | solution.py:140
  32.2 2.1 %collective-permute-done.3.rest_2_ = f32[1,128]{1,0:T(1,128)S(1)} collective-permute-done((f32[1,128]{1,0:T(1,128)S(1)}, f32[1,128]{1,0:T(1,128)S(1)}, u32[]{:S(2)}, u32[]{:S(2)}) %collective-permute-start.3) | collective-permute-done | bytes 544 | tf_op jit(solution)/shard_map/ppermute | solution.py:140
  34.4 0.6 %canopy_share.1 = f32[4,128]{1,0:T(4,128)} custom-call(f32[4,128]{1,0:T(4,128)S(1)} %get-tuple-element.11.grid_sum_ref, f32[1,128]{1,0:T(1,128)S(1)} %get-tuple-element.12.total_ref, f32[1,128]{1,0:T(1,128)S(1)} %collective-permute-done.1.rest_0_, f32[1,128]{1,0:T(1,128)S(1)} %collective-permute-done.2.rest_1_, f32[1,128]{1,0:T(1,128)S(1)} %collective-permute-done.3.rest_2_), custom_call_target="tpu_custom_call" | custom-call | tf_op jit(solution)/shard_map/canopy_share/pallas_call | solution.py:143
  (3 shorter events, 0.0 us)
Async XLA Ops:
  0.0 0.8 %copy-start = (f32[4,4096]{1,0:T(4,128)S(1)}, f32[4,4096]{1,0:T(4,128)}, u32[]{:S(2)}) copy-start(f32[4,4096]{1,0:T(4,128)} %weight_ref.1) | copy-start | bytes 196612
  0.8 0.7 %copy-start.2 = (s32[4096,1]{0,1:T(1,128)S(1)}, s32[4096,1]{0,1:T(1,128)}, u32[]{:S(2)}) copy-start(s32[4096,1]{0,1:T(1,128)} %param.12) | copy-start | bytes 49156
  1.6 0.7 %copy-start.3 = (s32[4096]{0:T(1024)S(1)}, s32[4096]{0:T(1024)}, u32[]{:S(2)}) copy-start(s32[4096]{0:T(1024)} %param.13) | copy-start | bytes 49156
  3.0 1.3 %collective-permute-start = (f32[128,128]{1,0:T(8,128)S(1)}, f32[128,128]{1,0:T(8,128)S(1)}, u32[]{:S(2)}, u32[]{:S(2)}) collective-permute-start(f32[128,128]{1,0:T(8,128)S(1)} %get-tuple-element.10), channel_id=1, source_target_pairs={{0,4},{4,0},{1,5},{5,1},{2,6},{6,2},{3,7},{7,3},{8,12},{12,8},{9,1... | collective-permute-start | bytes 196616 | tf_op jit(solution)/shard_map/ppermute | solution.py:123
  5.0 12.9 %copy-start.1 = (f32[12,4,128]{2,1,0:T(4,128)S(1)}, f32[12,4,128]{2,1,0:T(4,128)}, u32[]{:S(2)}) copy-start(f32[12,4,128]{2,1,0:T(4,128)} %leaf_ref.1) | copy-start | bytes 73732
  5.0 13.0 %copy-start.4 = (f32[10,128]{1,0:T(8,128)S(1)}, f32[10,128]{1,0:T(8,128)}, u32[]{:S(2)}) copy-start(f32[10,128]{1,0:T(8,128)} %soil_ref.1) | copy-start | bytes 15364
  5.0 21.6 %all-to-all-start = ((f32[32,4,128]{2,1,0:T(4,128)}), f32[32,4,128]{2,1,0:T(4,128)S(1)}, u32[]{:S(2)}, u32[]{:S(2)}) async-start(f32[32,4,128]{2,1,0:T(4,128)} %bitcast.3), calls=%async_computation | async-start | bytes 131072 | tf_op jit(solution)/shard_map/all_to_all | solution.py:124
  16.6 1.3 %copy-start.5 = (f32[4,10]{1,0:T(4,128)S(1)}, f32[4,10]{1,0:T(4,128)}, u32[]{:S(2)}) copy-start(f32[4,10]{1,0:T(4,128)} %root_ref.1) | copy-start | bytes 484
  26.6 3.6 %collective-permute-start.1 = (f32[1,128]{1,0:T(1,128)S(1)}, f32[1,128]{1,0:T(1,128)S(1)}, u32[]{:S(2)}, u32[]{:S(2)}) collective-permute-start(f32[1,128]{1,0:T(1,128)S(1)} %get-tuple-element.12.total_ref), channel_id=1, source_target_pairs={{0,1},{1,2},{2,3},{3,0},{4,5},{5,6},{6,7},{7,4},{8,9},{9,10},{10,1... | collective-permute-start | bytes 1544 | tf_op jit(solution)/shard_map/ppermute | solution.py:140
  27.2 5.0 %collective-permute-start.2 = (f32[1,128]{1,0:T(1,128)S(1)}, f32[1,128]{1,0:T(1,128)S(1)}, u32[]{:S(2)}, u32[]{:S(2)}) collective-permute-start(f32[1,128]{1,0:T(1,128)S(1)} %get-tuple-element.12.total_ref), channel_id=1, source_target_pairs={{0,2},{1,3},{2,0},{3,1},{4,6},{5,7},{6,4},{7,5},{8,10},{9,11},{10,... | collective-permute-start | bytes 1544 | tf_op jit(solution)/shard_map/ppermute | solution.py:140
  29.6 4.8 %collective-permute-start.3 = (f32[1,128]{1,0:T(1,128)S(1)}, f32[1,128]{1,0:T(1,128)S(1)}, u32[]{:S(2)}, u32[]{:S(2)}) collective-permute-start(f32[1,128]{1,0:T(1,128)S(1)} %get-tuple-element.12.total_ref), channel_id=1, source_target_pairs={{0,3},{1,0},{2,1},{3,2},{4,7},{5,4},{6,5},{7,6},{8,11},{9,8},{10,9... | collective-permute-start | bytes 1544 | tf_op jit(solution)/shard_map/ppermute | solution.py:140

commit v2 on v1

v2 whole, which is shorter than its diff:
```python
import jax
import jax.numpy as jnp
from jax import lax
from jax.experimental import pallas as pl
from jax.experimental.pallas import tpu as pltpu
from jax.sharding import PartitionSpec as P

F32 = jnp.float32
BF16 = jnp.bfloat16
CHUNK = 256
CELLS = 128


def vmem():
    return pl.BlockSpec(memory_space=pltpu.VMEM)


def smem():
    return pl.BlockSpec(memory_space=pltpu.SMEM)


def hbm():
    return pl.BlockSpec(memory_space=pltpu.HBM)


def limit(mib):
    return pltpu.CompilerParams(vmem_limit_bytes=mib << 20)


def load(pairs, sems):
    copies = [pltpu.make_async_copy(a, b, sems.at[i]) for i, (a, b) in enumerate(pairs)]
    for copy in copies:
        copy.start()
    return copies


def weight_sums_kernel(
    core_ref, weight_hbm, owner_hbm, local_hbm, send_ref, keep_ref,
    weight_ref, owner_ref, local_ref, sems,
):
    copies = load(
        [(weight_hbm, weight_ref), (owner_hbm, owner_ref), (local_hbm, local_ref)], sems
    )
    types, patches = weight_ref.shape
    rows = send_ref.shape[0]
    chips = rows // types
    row_chip = (lax.broadcasted_iota(jnp.int32, (rows, CHUNK), 0) // types + 22) % chips
    row_chip = row_chip.astype(F32).astype(BF16)
    column = lax.broadcasted_iota(jnp.int32, (2 * CELLS, CHUNK), 0).astype(F32).astype(BF16)
    zero = jnp.zeros((), BF16)
    one = jnp.ones((), BF16)
    total = jnp.zeros((2 * rows, 2 * CELLS), F32)
    for copy in copies:
        copy.wait()
    for step in range(patches // CHUNK):
        part = pl.ds(step * CHUNK, CHUNK)
        owner = owner_ref[:, part]
        chip = (owner >> 1).astype(F32).astype(BF16)
        place = ((owner & 1) * CELLS + local_ref[:, part]).astype(F32).astype(BF16)
        weight = weight_ref[:, part]
        high = weight.astype(BF16)
        low = (weight - high.astype(F32)).astype(BF16)
        named = jnp.broadcast_to(chip, (rows, CHUNK)) == row_chip
        left = jnp.concatenate(
            [
                jnp.where(named, jnp.concatenate([high] * chips, axis=0), zero),
                jnp.where(named, jnp.concatenate([low] * chips, axis=0), zero),
            ],
            axis=0,
        )
        right = jnp.where(jnp.broadcast_to(place, (2 * CELLS, CHUNK)) == column, one, zero)
        total += lax.dot_general(
            left, right, (((1,), (1,)), ((), ())), preferred_element_type=F32
        )
    both = total[:rows] + total[rows:]
    first, second = both[:, :CELLS], both[:, CELLS:]
    low_core = core_ref[0] == 0
    send_ref[...] = jnp.where(low_core, second, first)
    keep_ref[...] = jnp.where(low_core, first, second)


def weight_sums(core, arrays, chips):
    types = arrays[0].shape[0]
    shape = jax.ShapeDtypeStruct((chips * types, CELLS), F32)
    return pl.pallas_call(
        weight_sums_kernel,
        out_shape=[shape, shape],
        in_specs=[smem()] + [hbm()] * len(arrays),
        out_specs=[vmem()] * 2,
        scratch_shapes=[pltpu.VMEM(a.shape, a.dtype) for a in arrays]
        + [pltpu.SemaphoreType.DMA((len(arrays),))],
        compiler_params=limit(8),
        name="weight_sums",
    )(core, *[pltpu.with_memory_space_constraint(a, pltpu.HBM) for a in arrays])


def factor_kernel(month_ref, mix_ref, leaf_ref, soil_ref, root_ref, factor_ref):
    earlier = month_ref[0]
    later = jnp.where(earlier == leaf_ref.shape[0] - 1, 0, earlier + 1)
    mix = mix_ref[0]
    current = mix * leaf_ref[earlier] + (1.0 - mix) * leaf_ref[later]
    stress = jnp.zeros_like(current)
    for layer in range(soil_ref.shape[0]):
        stress += root_ref[:, layer : layer + 1] * soil_ref[layer : layer + 1, :]
    factor_ref[...] = (1.0 - jnp.exp(-0.5 * current)) * stress


def cell_factor(month, mix, leaf_area, soil_water, root_share):
    return pl.pallas_call(
        factor_kernel,
        out_shape=jax.ShapeDtypeStruct(leaf_area.shape[1:], F32),
        in_specs=[smem(), smem(), vmem(), vmem(), vmem()],
        out_specs=vmem(),
        compiler_params=limit(1),
        cost_estimate=pl.CostEstimate(flops=20000, transcendentals=512, bytes_accessed=40000),
        name="cell_factor",
    )(month, mix, leaf_area, soil_water, root_share)


def grid_sum_kernel(received_ref, factor_ref, grid_sum_ref, total_ref):
    grid_sum = jnp.sum(received_ref[...], axis=0) * factor_ref[...]
    grid_sum_ref[...] = grid_sum
    total_ref[...] = jnp.broadcast_to(jnp.sum(grid_sum, axis=0, keepdims=True)[None], total_ref.shape)


def share_kernel(grid_sum_ref, totals_ref, share_ref):
    share_ref[...] = grid_sum_ref[...] / (1.0 + jnp.sum(totals_ref[...], axis=0))


def on_device(
    leaf_area, soil_water, root_share, patch_weight, patch_owner, patch_local, month, mix
):
    types = leaf_area.shape[1]
    devices = lax.axis_size("blk")
    chips = devices // 2
    layers = lax.axis_size("layer")
    core = (lax.axis_index("blk").astype(jnp.int32) & 1).reshape(1)
    send, keep = weight_sums(
        core, [patch_weight, patch_owner.reshape(1, -1), patch_local.reshape(1, -1)], chips
    )
    factor = cell_factor(month, mix, leaf_area, soil_water, root_share)
    sums = keep + lax.ppermute(send, "blk", [(i, i ^ 1) for i in range(devices)])
    sums, factor = lax.optimization_barrier((sums, factor))
    received = lax.all_to_all(
        sums.reshape(chips, types, CELLS), "blk", split_axis=0, concat_axis=0, tiled=True,
        axis_index_groups=[
            [(i + 22) % chips * 2 + half for i in range(chips)] for half in range(2)
        ],
    )
    grid_sum, total = pl.pallas_call(
        grid_sum_kernel,
        out_shape=[
            jax.ShapeDtypeStruct((types, CELLS), F32),
            jax.ShapeDtypeStruct((layers, 1, CELLS), F32),
        ],
        in_specs=[vmem(), vmem()],
        out_specs=[vmem(), vmem()],
        compiler_params=limit(1),
        name="grid_sum",
    )(received, factor)
    totals = lax.all_to_all(
        total, "layer", split_axis=0, concat_axis=0, tiled=True,
        axis_index_groups=[[(i + 2) % layers for i in range(layers)]],
    )
    operands = [grid_sum, totals]
    return pl.pallas_call(
        share_kernel,
        out_shape=jax.ShapeDtypeStruct((types, CELLS), F32),
        in_specs=[vmem()] * len(operands),
        out_specs=vmem(),
        compiler_params=limit(1),
        name="canopy_share",
    )(*operands)


def solution(mesh):
    in_specs = (
        P(None, "layer", "blk"),
        P(None, "blk"),
        P("layer", None),
        P("layer", "blk"),
        P("blk", None),
        P("blk"),
        P(),
        P(),
    )
    return jax.shard_map(
        on_device, mesh=mesh, in_specs=in_specs, out_specs=P("layer", "blk"), check_vma=False
    )
```

time: 35.3 us -> 28.3 us (0.80)
  the two profiles are of different devices: /device:TPU:6 before, /device:TPU:8 now
where the time goes in v2:
time: 28.3 us; the launch traced here: 28 us
  blocking collectives  24.2 us (86%)
  Pallas kernels  2.34 us (8%)
  between operations  1.36 us (5%)
    all_to_all x1, blocking collectives, on_device(): lax.all_to_all(sums.reshape(chips, types, CELLS), 'blk', split_axis=0, co...  16.5 us
    all_to_all x1, blocking collectives, on_device(): lax.all_to_all(total, 'layer', split_axis=0, concat_axis=0, tiled=True, a...  7.65 us
    pallas_call x1, Pallas kernels, weight_sums(): pl.pallas_call(weight_sums_kernel, out_shape=[shape, shape], in_specs=[sm...  1.62 us
    pallas_call x1, Pallas kernels, on_device(): pl.pallas_call(share_kernel, out_shape=jax.ShapeDtypeStruct((types, CELLS...  0.59 us
  transfers between devices with their start and end apart: 1, of which 0 were waited for; matrix products, arithmetic and copies ran while one was open for 0% of the time, Pallas kernels for 0%

profile of v2, /device:TPU:8, one launch (start us, length us, event | category | flops | bytes accessed | tf_op | source)
XLA Modules:
  0.0 28.0 jit_solution(14348952252818649331)
XLA Ops:
  0.0 0.0 copy-start
  0.0 0.0 copy-start.1
  0.0 1.6 %weight_sums.1 = (f32[128,128]{1,0:T(8,128)S(1)}, f32[128,128]{1,0:T(8,128)S(1)}) custom-call(s32[1]{0:T(128)} %bitcast.core_ref, f32[4,4096]{1,0:T(4,128)} %weight_hbm.1, s32[1,4096]{1,0:T(1,128)} %bitcast.5, s32[1,4096]{1,0:T(1,128)} %bitcast.6), custom_call_target="tpu_custom_call" | custom-call | tf_op jit(solution)/shard_map/weight_sums/pallas_call | solution.py:85
  1.6 0.0 copy-start.2
  1.6 0.1 collective-permute-start
  3.0 0.0 copy-done
  3.0 0.0 copy-done.1
  3.1 0.0 copy-done.2
  3.1 0.1 cell_factor.1.factor_ref
  3.2 0.0 collective-permute-done
  3.2 16.5 %all_to_all.10.received_ref = f32[32,4,128]{2,1,0:T(4,128)S(1)} all-to-all(f32[32,4,128]{2,1,0:T(4,128)S(1)} %bitcast.4), channel_id=1, replica_groups={{176,184,192,200,208,216,224,232,240,248,0,8,16,24,32,40,48,56,64,72,80..., dimensions={0} | all-to-all | bytes 131072 | tf_op jit(solution)/shard_map/all_to_all | solution.py:144
  19.7 7.6 %all_to_all.11.totals_ref = f32[4,1,128]{2,1,0:T(1,128)S(1)} all-to-all(f32[4,1,128]{2,1,0:T(1,128)S(1)} %get-tuple-element.16), channel_id=1, replica_groups={{2,3,0,1},{6,7,4,5},{10,11,8,9},{14,15,12,13},{18,19,16,17},{22,23,20,2..., dimensions={0} | all-to-all | bytes 4096 | tf_op jit(solution)/shard_map/all_to_all | solution.py:161
  27.4 0.6 %canopy_share.1 = f32[4,128]{1,0:T(4,128)} custom-call(f32[4,128]{1,0:T(4,128)S(1)} %get-tuple-element.15.grid_sum_ref, f32[4,1,128]{2,1,0:T(1,128)S(1)} %all_to_all.11.totals_ref), custom_call_target="tpu_custom_call" | custom-call | tf_op jit(solution)/shard_map/canopy_share/pallas_call | solution.py:166
  (2 shorter events, 0.1 us)
Async XLA Ops:
  0.0 3.0 %copy-start = (f32[12,4,128]{2,1,0:T(4,128)S(1)}, f32[12,4,128]{2,1,0:T(4,128)}, u32[]{:S(2)}) copy-start(f32[12,4,128]{2,1,0:T(4,128)} %leaf_ref.1) | copy-start | bytes 73732
  0.0 3.0 %copy-start.1 = (f32[10,128]{1,0:T(8,128)S(1)}, f32[10,128]{1,0:T(8,128)}, u32[]{:S(2)}) copy-start(f32[10,128]{1,0:T(8,128)} %soil_ref.1) | copy-start | bytes 15364
  1.6 1.4 %copy-start.2 = (f32[4,10]{1,0:T(4,128)S(1)}, f32[4,10]{1,0:T(4,128)}, u32[]{:S(2)}) copy-start(f32[4,10]{1,0:T(4,128)} %root_ref.1) | copy-start | bytes 484
  1.6 1.5 %collective-permute-start = (f32[128,128]{1,0:T(8,128)S(1)}, f32[128,128]{1,0:T(8,128)S(1)}, u32[]{:S(2)}, u32[]{:S(2)}) collective-permute-start(f32[128,128]{1,0:T(8,128)S(1)} %get-tuple-element.12), channel_id=1, source_target_pairs={{0,4},{4,0},{8,12},{12,8},{16,20},{20,16},{24,28},{28,24},{32,36},... | collective-permute-start | bytes 196616 | tf_op jit(solution)/shard_map/ppermute | solution.py:142

commit v3 on v2

--- a/solution.py
+++ b/solution.py
@@ -120,11 +120,15 @@
 def grid_sum_kernel(received_ref, factor_ref, grid_sum_ref, total_ref):
     grid_sum = jnp.sum(received_ref[...], axis=0) * factor_ref[...]
     grid_sum_ref[...] = grid_sum
-    total_ref[...] = jnp.broadcast_to(jnp.sum(grid_sum, axis=0, keepdims=True)[None], total_ref.shape)
+    total_ref[...] = jnp.sum(grid_sum, axis=0, keepdims=True)
 
 
-def share_kernel(grid_sum_ref, totals_ref, share_ref):
-    share_ref[...] = grid_sum_ref[...] / (1.0 + jnp.sum(totals_ref[...], axis=0))
+def share_kernel(grid_sum_ref, total_ref, *rest):
+    *others, share_ref = rest
+    total = total_ref[...]
+    for other in others:
+        total += other[...]
+    share_ref[...] = grid_sum_ref[...] / (1.0 + total)
 
 
 def on_device(
@@ -151,18 +155,17 @@
         grid_sum_kernel,
         out_shape=[
             jax.ShapeDtypeStruct((types, CELLS), F32),
-            jax.ShapeDtypeStruct((layers, 1, CELLS), F32),
+            jax.ShapeDtypeStruct((1, CELLS), F32),
         ],
         in_specs=[vmem(), vmem()],
         out_specs=[vmem(), vmem()],
         compiler_params=limit(1),
         name="grid_sum",
     )(received, factor)
-    totals = lax.all_to_all(
-        total, "layer", split_axis=0, concat_axis=0, tiled=True,
-        axis_index_groups=[[(i + 2) % layers for i in range(layers)]],
-    )
-    operands = [grid_sum, totals]
+    others = [
+        lax.ppermute(total, "layer", pairs) for pairs in [[(0, 3), (1, 2), (2, 0), (3, 1)], [(0, 2), (1, 3), (2, 1), (3, 0)], [(0, 1), (1, 0), (2, 3), (3, 2)]]
+    ]
+    operands = [grid_sum, total, *others]
     return pl.pallas_call(
         share_kernel,
         out_shape=jax.ShapeDtypeStruct((types, CELLS), F32),

time: 28.3 us -> 28.1 us (level)
  blocking collectives: 24.2 us -> 16.5 us
  starting transfers between devices: 0.09 us -> 5.19 us
  waiting for transfers between devices: 0.01 us -> 2.47 us
    all_to_all x1 -> x0, blocking collectives: 7.65 us -> none  [on_device(): lax.all_to_all(total, 'layer', split_axis=0, concat_axis=0, tiled=True, a...]
    ppermute x0 -> x3, starting transfers between devices: none -> 5.09 us  [on_device(): lax.ppermute(total, 'layer', pairs)]
    ppermute x0 -> x3, waiting for transfers between devices: none -> 2.47 us  [on_device(): lax.ppermute(total, 'layer', pairs)]
  transfers between devices with their start and end apart: 1 -> 4, of which waited for: 0 -> 1; matrix products, arithmetic and copies ran while one was open for 0% -> 0% of each run, Pallas kernels for 0% -> 0%
where the time goes in v3:
time: 28.1 us; the launch traced here: 27.9 us
  blocking collectives  16.5 us (59%)
  starting transfers between devices  5.19 us (18%)
  waiting for transfers between devices  2.47 us (9%)
  Pallas kernels  2.34 us (8%)
  between operations  1.36 us (5%)
    all_to_all x1, blocking collectives, on_device(): lax.all_to_all(sums.reshape(chips, types, CELLS), 'blk', split_axis=0, co...  16.5 us
    ppermute x3, starting transfers between devices, on_device(): lax.ppermute(total, 'layer', pairs)  5.09 us
    ppermute x3, waiting for transfers between devices, on_device(): lax.ppermute(total, 'layer', pairs)  2.47 us
    pallas_call x1, Pallas kernels, weight_sums(): pl.pallas_call(weight_sums_kernel, out_shape=[shape, shape], in_specs=[sm...  1.62 us
    pallas_call x1, Pallas kernels, on_device(): pl.pallas_call(share_kernel, out_shape=jax.ShapeDtypeStruct((types, CELLS...  0.59 us
  transfers between devices with their start and end apart: 4, of which 1 were waited for; matrix products, arithmetic and copies ran while one was open for 0% of the time, Pallas kernels for 0%

profile of v3, /device:TPU:8, one launch (start us, length us, event | category | flops | bytes accessed | tf_op | source)
XLA Modules:
  0.0 27.9 jit_solution(14253412157105620261)
XLA Ops:
  0.0 0.0 copy-start
  0.0 0.0 copy-start.1
  0.0 1.6 %weight_sums.1 = (f32[128,128]{1,0:T(8,128)S(1)}, f32[128,128]{1,0:T(8,128)S(1)}) custom-call(s32[1]{0:T(128)} %bitcast.core_ref, f32[4,4096]{1,0:T(4,128)} %weight_hbm.1, s32[1,4096]{1,0:T(1,128)} %bitcast.5, s32[1,4096]{1,0:T(1,128)} %bitcast.6), custom_call_target="tpu_custom_call" | custom-call | tf_op jit(solution)/shard_map/weight_sums/pallas_call | solution.py:85
  1.6 0.0 copy-start.2
  1.6 0.1 collective-permute-start
  3.0 0.0 copy-done
  3.0 0.0 copy-done.1
  3.1 0.0 copy-done.2
  3.1 0.1 cell_factor.1.factor_ref
  3.2 0.0 collective-permute-done
  3.2 16.5 %all_to_all.5.received_ref = f32[32,4,128]{2,1,0:T(4,128)S(1)} all-to-all(f32[32,4,128]{2,1,0:T(4,128)S(1)} %bitcast.4), channel_id=1, replica_groups={{176,184,192,200,208,216,224,232,240,248,0,8,16,24,32,40,48,56,64,72,80..., dimensions={0} | all-to-all | bytes 131072 | tf_op jit(solution)/shard_map/all_to_all | solution.py:148
  19.7 2.8 %collective-permute-start.1 = (f32[1,128]{1,0:T(1,128)S(1)}, f32[1,128]{1,0:T(1,128)S(1)}, u32[]{:S(2)}, u32[]{:S(2)}) collective-permute-start(f32[1,128]{1,0:T(1,128)S(1)} %get-tuple-element.16.total_ref), channel_id=1, source_target_pairs={{0,3},{1,2},{2,0},{3,1},{4,7},{5,6},{6,4},{7,5},{8,11},{9,10},{10,... | collective-permute-start | bytes 1544 | tf_op jit(solution)/shard_map/ppermute | solution.py:166
  22.5 0.8 %collective-permute-start.2 = (f32[1,128]{1,0:T(1,128)S(1)}, f32[1,128]{1,0:T(1,128)S(1)}, u32[]{:S(2)}, u32[]{:S(2)}) collective-permute-start(f32[1,128]{1,0:T(1,128)S(1)} %get-tuple-element.16.total_ref), channel_id=1, source_target_pairs={{0,2},{1,3},{2,1},{3,0},{4,6},{5,7},{6,5},{7,4},{8,10},{9,11},{10,... | collective-permute-start | bytes 1544 | tf_op jit(solution)/shard_map/ppermute | solution.py:166
  23.3 1.5 %collective-permute-start.3 = (f32[1,128]{1,0:T(1,128)S(1)}, f32[1,128]{1,0:T(1,128)S(1)}, u32[]{:S(2)}, u32[]{:S(2)}) collective-permute-start(f32[1,128]{1,0:T(1,128)S(1)} %get-tuple-element.16.total_ref), channel_id=1, source_target_pairs={{0,1},{1,0},{2,3},{3,2},{4,5},{5,4},{6,7},{7,6},{8,9},{9,8},{10,11... | collective-permute-start | bytes 1544 | tf_op jit(solution)/shard_map/ppermute | solution.py:166
  24.8 0.0 collective-permute-done.1.rest_0_
  24.9 2.4 %collective-permute-done.2.rest_1_ = f32[1,128]{1,0:T(1,128)S(1)} collective-permute-done((f32[1,128]{1,0:T(1,128)S(1)}, f32[1,128]{1,0:T(1,128)S(1)}, u32[]{:S(2)}, u32[]{:S(2)}) %collective-permute-start.2) | collective-permute-done | bytes 544 | tf_op jit(solution)/shard_map/ppermute | solution.py:166
  27.3 0.0 collective-permute-done.3.rest_2_
  27.3 0.6 %canopy_share.1 = f32[4,128]{1,0:T(4,128)} custom-call(f32[4,128]{1,0:T(4,128)S(1)} %get-tuple-element.15.grid_sum_ref, f32[1,128]{1,0:T(1,128)S(1)} %get-tuple-element.16.total_ref, f32[1,128]{1,0:T(1,128)S(1)} %collective-permute-done.1.rest_0_, f32[1,128]{1,0:T(1,128)S(1)} %collective-permute-done.2.rest_1_, f32[1,128]{1,0:T(1,128)S(1)} %collective-permute-done.3.rest_2_), custom_call_target="tpu_custom_call" | custom-call | tf_op jit(solution)/shard_map/canopy_share/pallas_call | solution.py:169
  (2 shorter events, 0.1 us)
Async XLA Ops:
  0.0 3.0 %copy-start = (f32[12,4,128]{2,1,0:T(4,128)S(1)}, f32[12,4,128]{2,1,0:T(4,128)}, u32[]{:S(2)}) copy-start(f32[12,4,128]{2,1,0:T(4,128)} %leaf_ref.1) | copy-start | bytes 73732
  0.0 3.0 %copy-start.1 = (f32[10,128]{1,0:T(8,128)S(1)}, f32[10,128]{1,0:T(8,128)}, u32[]{:S(2)}) copy-start(f32[10,128]{1,0:T(8,128)} %soil_ref.1) | copy-start | bytes 15364
  1.6 1.4 %copy-start.2 = (f32[4,10]{1,0:T(4,128)S(1)}, f32[4,10]{1,0:T(4,128)}, u32[]{:S(2)}) copy-start(f32[4,10]{1,0:T(4,128)} %root_ref.1) | copy-start | bytes 484
  1.6 1.5 %collective-permute-start = (f32[128,128]{1,0:T(8,128)S(1)}, f32[128,128]{1,0:T(8,128)S(1)}, u32[]{:S(2)}, u32[]{:S(2)}) collective-permute-start(f32[128,128]{1,0:T(8,128)S(1)} %get-tuple-element.12), channel_id=1, source_target_pairs={{0,4},{4,0},{8,12},{12,8},{16,20},{20,16},{24,28},{28,24},{32,36},... | collective-permute-start | bytes 196616 | tf_op jit(solution)/shard_map/ppermute | solution.py:146
  19.7 5.1 %collective-permute-start.1 = (f32[1,128]{1,0:T(1,128)S(1)}, f32[1,128]{1,0:T(1,128)S(1)}, u32[]{:S(2)}, u32[]{:S(2)}) collective-permute-start(f32[1,128]{1,0:T(1,128)S(1)} %get-tuple-element.16.total_ref), channel_id=1, source_target_pairs={{0,3},{1,2},{2,0},{3,1},{4,7},{5,6},{6,4},{7,5},{8,11},{9,10},{10,... | collective-permute-start | bytes 1544 | tf_op jit(solution)/shard_map/ppermute | solution.py:166
  22.5 4.8 %collective-permute-start.2 = (f32[1,128]{1,0:T(1,128)S(1)}, f32[1,128]{1,0:T(1,128)S(1)}, u32[]{:S(2)}, u32[]{:S(2)}) collective-permute-start(f32[1,128]{1,0:T(1,128)S(1)} %get-tuple-element.16.total_ref), channel_id=1, source_target_pairs={{0,2},{1,3},{2,1},{3,0},{4,6},{5,7},{6,5},{7,4},{8,10},{9,11},{10,... | collective-permute-start | bytes 1544 | tf_op jit(solution)/shard_map/ppermute | solution.py:166
  23.3 4.0 %collective-permute-start.3 = (f32[1,128]{1,0:T(1,128)S(1)}, f32[1,128]{1,0:T(1,128)S(1)}, u32[]{:S(2)}, u32[]{:S(2)}) collective-permute-start(f32[1,128]{1,0:T(1,128)S(1)} %get-tuple-element.16.total_ref), channel_id=1, source_target_pairs={{0,1},{1,0},{2,3},{3,2},{4,5},{5,4},{6,7},{7,6},{8,9},{9,8},{10,11... | collective-permute-start | bytes 1544 | tf_op jit(solution)/shard_map/ppermute | solution.py:166

commit v4 on v3

--- a/solution.py
+++ b/solution.py
@@ -162,8 +162,18 @@
         compiler_params=limit(1),
         name="grid_sum",
     )(received, factor)
+    orders = ((3, 2, 0, 1), (2, 3, 1, 0), (1, 0, 3, 2))
     others = [
-        lax.ppermute(total, "layer", pairs) for pairs in [[(0, 3), (1, 2), (2, 0), (3, 1)], [(0, 2), (1, 3), (2, 1), (3, 0)], [(0, 1), (1, 0), (2, 3), (3, 2)]]
+        lax.ppermute(
+            total,
+            ("blk", "layer"),
+            [
+                (i * layers + x, i * layers + orders[(step + i % 2 * 2) % 3][x])
+                for i in range(devices)
+                for x in range(layers)
+            ],
+        )
+        for step in range(3)
     ]
     operands = [grid_sum, total, *others]
     return pl.pallas_call(

time: 28.1 us -> 28.1 us (level)
  no operation moved by 1% of the time
where the time goes in v4:
time: 28.1 us; the launch traced here: 27.9 us
  blocking collectives  16.5 us (59%)
  starting transfers between devices  5.19 us (18%)
  waiting for transfers between devices  2.47 us (9%)
  Pallas kernels  2.34 us (8%)
  between operations  1.36 us (5%)
    all_to_all x1, blocking collectives, on_device(): lax.all_to_all(sums.reshape(chips, types, CELLS), 'blk', split_axis=0, co...  16.5 us
    ppermute x3, starting transfers between devices, on_device(): lax.ppermute(total, ('blk', 'layer'), [(i * layers + x, i * layers + orde...  5.09 us
    ppermute x3, waiting for transfers between devices, on_device(): lax.ppermute(total, ('blk', 'layer'), [(i * layers + x, i * layers + orde...  2.47 us
    pallas_call x1, Pallas kernels, weight_sums(): pl.pallas_call(weight_sums_kernel, out_shape=[shape, shape], in_specs=[sm...  1.62 us
    pallas_call x1, Pallas kernels, on_device(): pl.pallas_call(share_kernel, out_shape=jax.ShapeDtypeStruct((types, CELLS...  0.59 us
  transfers between devices with their start and end apart: 4, of which 1 were waited for; matrix products, arithmetic and copies ran while one was open for 0% of the time, Pallas kernels for 0%

profile of v4, /device:TPU:8, one launch (start us, length us, event | category | flops | bytes accessed | tf_op | source)
XLA Modules:
  0.0 27.9 jit_solution(18031825807055367153)
XLA Ops:
  0.0 0.0 copy-start
  0.0 0.0 copy-start.1
  0.0 1.6 %weight_sums.1 = (f32[128,128]{1,0:T(8,128)S(1)}, f32[128,128]{1,0:T(8,128)S(1)}) custom-call(s32[1]{0:T(128)} %bitcast.core_ref, f32[4,4096]{1,0:T(4,128)} %weight_hbm.1, s32[1,4096]{1,0:T(1,128)} %bitcast.5, s32[1,4096]{1,0:T(1,128)} %bitcast.6), custom_call_target="tpu_custom_call" | custom-call | tf_op jit(solution)/shard_map/weight_sums/pallas_call | solution.py:85
  1.6 0.0 copy-start.2
  1.6 0.1 collective-permute-start
  3.0 0.0 copy-done
  3.0 0.0 copy-done.1
  3.1 0.0 copy-done.2
  3.1 0.1 cell_factor.1.factor_ref
  3.2 0.0 collective-permute-done
  3.2 16.5 %all_to_all.5.received_ref = f32[32,4,128]{2,1,0:T(4,128)S(1)} all-to-all(f32[32,4,128]{2,1,0:T(4,128)S(1)} %bitcast.4), channel_id=1, replica_groups={{176,184,192,200,208,216,224,232,240,248,0,8,16,24,32,40,48,56,64,72,80..., dimensions={0} | all-to-all | bytes 131072 | tf_op jit(solution)/shard_map/all_to_all | solution.py:148
  19.7 2.8 %collective-permute-start.1 = (f32[1,128]{1,0:T(1,128)S(1)}, f32[1,128]{1,0:T(1,128)S(1)}, u32[]{:S(2)}, u32[]{:S(2)}) collective-permute-start(f32[1,128]{1,0:T(1,128)S(1)} %get-tuple-element.16.total_ref), channel_id=1, source_target_pairs={{0,3},{1,2},{2,0},{3,1},{4,5},{5,4},{6,7},{7,6},{8,11},{9,10},{10,... | collective-permute-start | bytes 1544 | tf_op jit(solution)/shard_map/ppermute | solution.py:167
  22.5 0.8 %collective-permute-start.2 = (f32[1,128]{1,0:T(1,128)S(1)}, f32[1,128]{1,0:T(1,128)S(1)}, u32[]{:S(2)}, u32[]{:S(2)}) collective-permute-start(f32[1,128]{1,0:T(1,128)S(1)} %get-tuple-element.16.total_ref), channel_id=1, source_target_pairs={{0,2},{1,3},{2,1},{3,0},{4,7},{5,6},{6,4},{7,5},{8,10},{9,11},{10,... | collective-permute-start | bytes 1544 | tf_op jit(solution)/shard_map/ppermute | solution.py:167
  23.3 1.5 %collective-permute-start.3 = (f32[1,128]{1,0:T(1,128)S(1)}, f32[1,128]{1,0:T(1,128)S(1)}, u32[]{:S(2)}, u32[]{:S(2)}) collective-permute-start(f32[1,128]{1,0:T(1,128)S(1)} %get-tuple-element.16.total_ref), channel_id=1, source_target_pairs={{0,1},{1,0},{2,3},{3,2},{4,6},{5,7},{6,5},{7,4},{8,9},{9,8},{10,11... | collective-permute-start | bytes 1544 | tf_op jit(solution)/shard_map/ppermute | solution.py:167
  24.8 0.0 collective-permute-done.1.rest_0_
  24.9 2.4 %collective-permute-done.2.rest_1_ = f32[1,128]{1,0:T(1,128)S(1)} collective-permute-done((f32[1,128]{1,0:T(1,128)S(1)}, f32[1,128]{1,0:T(1,128)S(1)}, u32[]{:S(2)}, u32[]{:S(2)}) %collective-permute-start.2) | collective-permute-done | bytes 544 | tf_op jit(solution)/shard_map/ppermute | solution.py:167
  27.3 0.0 collective-permute-done.3.rest_2_
  27.3 0.6 %canopy_share.1 = f32[4,128]{1,0:T(4,128)} custom-call(f32[4,128]{1,0:T(4,128)S(1)} %get-tuple-element.15.grid_sum_ref, f32[1,128]{1,0:T(1,128)S(1)} %get-tuple-element.16.total_ref, f32[1,128]{1,0:T(1,128)S(1)} %collective-permute-done.1.rest_0_, f32[1,128]{1,0:T(1,128)S(1)} %collective-permute-done.2.rest_1_, f32[1,128]{1,0:T(1,128)S(1)} %collective-permute-done.3.rest_2_), custom_call_target="tpu_custom_call" | custom-call | tf_op jit(solution)/shard_map/canopy_share/pallas_call | solution.py:179
  (2 shorter events, 0.1 us)
Async XLA Ops:
  0.0 3.0 %copy-start = (f32[12,4,128]{2,1,0:T(4,128)S(1)}, f32[12,4,128]{2,1,0:T(4,128)}, u32[]{:S(2)}) copy-start(f32[12,4,128]{2,1,0:T(4,128)} %leaf_ref.1) | copy-start | bytes 73732
  0.0 3.0 %copy-start.1 = (f32[10,128]{1,0:T(8,128)S(1)}, f32[10,128]{1,0:T(8,128)}, u32[]{:S(2)}) copy-start(f32[10,128]{1,0:T(8,128)} %soil_ref.1) | copy-start | bytes 15364
  1.6 1.4 %copy-start.2 = (f32[4,10]{1,0:T(4,128)S(1)}, f32[4,10]{1,0:T(4,128)}, u32[]{:S(2)}) copy-start(f32[4,10]{1,0:T(4,128)} %root_ref.1) | copy-start | bytes 484
  1.6 1.5 %collective-permute-start = (f32[128,128]{1,0:T(8,128)S(1)}, f32[128,128]{1,0:T(8,128)S(1)}, u32[]{:S(2)}, u32[]{:S(2)}) collective-permute-start(f32[128,128]{1,0:T(8,128)S(1)} %get-tuple-element.12), channel_id=1, source_target_pairs={{0,4},{4,0},{8,12},{12,8},{16,20},{20,16},{24,28},{28,24},{32,36},... | collective-permute-start | bytes 196616 | tf_op jit(solution)/shard_map/ppermute | solution.py:146
  19.7 5.1 %collective-permute-start.1 = (f32[1,128]{1,0:T(1,128)S(1)}, f32[1,128]{1,0:T(1,128)S(1)}, u32[]{:S(2)}, u32[]{:S(2)}) collective-permute-start(f32[1,128]{1,0:T(1,128)S(1)} %get-tuple-element.16.total_ref), channel_id=1, source_target_pairs={{0,3},{1,2},{2,0},{3,1},{4,5},{5,4},{6,7},{7,6},{8,11},{9,10},{10,... | collective-permute-start | bytes 1544 | tf_op jit(solution)/shard_map/ppermute | solution.py:167
  22.5 4.8 %collective-permute-start.2 = (f32[1,128]{1,0:T(1,128)S(1)}, f32[1,128]{1,0:T(1,128)S(1)}, u32[]{:S(2)}, u32[]{:S(2)}) collective-permute-start(f32[1,128]{1,0:T(1,128)S(1)} %get-tuple-element.16.total_ref), channel_id=1, source_target_pairs={{0,2},{1,3},{2,1},{3,0},{4,7},{5,6},{6,4},{7,5},{8,10},{9,11},{10,... | collective-permute-start | bytes 1544 | tf_op jit(solution)/shard_map/ppermute | solution.py:167
  23.3 4.0 %collective-permute-start.3 = (f32[1,128]{1,0:T(1,128)S(1)}, f32[1,128]{1,0:T(1,128)S(1)}, u32[]{:S(2)}, u32[]{:S(2)}) collective-permute-start(f32[1,128]{1,0:T(1,128)S(1)} %get-tuple-element.16.total_ref), channel_id=1, source_target_pairs={{0,1},{1,0},{2,3},{3,2},{4,6},{5,7},{6,5},{7,4},{8,9},{9,8},{10,11... | collective-permute-start | bytes 1544 | tf_op jit(solution)/shard_map/ppermute | solution.py:167
